TPU v7x, 256 devices: a whole 4x4x8 slice. The times are simulated.
256 devices in a mesh: seq: 64 (over y, z, core), head: 4 (over x).
Axes of the slice: x: 4, y: 4, z: 8, core: 2. Of those that a mesh axis runs over, the one named last changes fastest.
Arguments:
- inner_input: bfloat16 [16384, 8192], P('seq', 'head'), may hold values from -6 to 6
- state_input: bfloat16 [16384, 2, 1024], P('seq', None, 'head'), may hold values from -3 to 3
- gate_input: bfloat16 [16384, 8192], P('seq', 'head'), may hold values from -6 to 6
- step_input: float32 [128, 16384], P('head', 'seq'), may hold values from -4.7 to 0.6
- decay_exponent: float32 [128], P('head')
- skip_gain: float32 [128], P('head'), may hold values from 0.5 to 1.5
- documents: int32 [16384], P('seq'), may hold values from 0 to 15, never falling along the last dimension, each value on 1 to 1536 neighbouring positions
- filter_inner: float32 [4, 8192], P(None, 'head'), may hold values from -3 to 3
- filter_state: float32 [4, 2, 1024], P(None, None, 'head'), may hold values from -3 to 3
- norm_gain: float32 [8192], P('head'), may hold values from 0.1 to 1.9
- output_weight: bfloat16 [8192, 4096], P('head', 'seq'), may hold values from -0.0625 to 0.0625
Outputs:
- mixed: bfloat16 [16384, 4096], P('seq', 'head')
Inputs may be any that keep to these rules, and one draw needn't show every extreme that they name: `documents`: document numbers never fall along the sequence.
All inputs are finite; a program needn't handle non-finite values.
Results may differ from a plain program's by a relative error of at most 0.0058.
Values may be sent and summed in bfloat16 or wider, within the bound.
No kernel may reach another device: no remote copies, remote signals or barrier semaphores. Data moves between devices by JAX's collectives and lax.ppermute only.
A program may use at most 192 MiB of HBM per device.

v0:
```python
import jax
import jax.numpy as jnp
from jax import lax
from jax.sharding import PartitionSpec as P

HEAD_DIM = 64
STATE = 128
GROUPS = 8
INNER = 8192
KERNEL = 4
SPAN = 256
DOC_MOST = 1536
REACH = -(-(DOC_MOST - 1) // SPAN)
highest = lax.Precision.HIGHEST


def passed_along(value, axis, steps):
    count = lax.axis_size(axis)
    initial, last = (max(0, -steps), min(count, count - steps))
    return lax.ppermute(value, axis, [(source, source + steps) for source in range(initial, last)])


def causal_conv(extended, weights, segments_wide, segment_block):
    length = segment_block.shape[0]
    running = jnp.zeros(extended[:length].shape, jnp.float32)
    for offset in range(KERNEL):
        window = extended[offset : offset + length].astype(jnp.float32)
        matches = segments_wide[offset : offset + length] == segment_block
        matches = matches.reshape((length,) + (1,) * (extended.ndim - 1))
        running = running + jnp.where(matches, window * weights[offset], jnp.float32(0.0))
    return jax.nn.silu(running).astype(jnp.bfloat16)


def span_parts(values, write_rows, read_rows, step_size, decay_rate, segment_block, prior_segment):
    length = segment_block.shape[0]
    repeat = decay_rate.shape[0] // write_rows.shape[1]
    cumulative = jnp.cumsum(decay_rate, axis=1)
    places = jnp.arange(length)
    linked = (segment_block[:, None] == segment_block[None, :]) & (
        places[:, None] >= places[None, :]
    )
    spread = cumulative[:, :, None] - cumulative[:, None, :]
    decays = jnp.exp(jnp.where(linked[None], spread, -jnp.inf))
    scores = jnp.einsum("ign,jgn->gij", read_rows, write_rows, preferred_element_type=jnp.float32)
    scores = jnp.repeat(scores, repeat, axis=0)
    mixing = (decays * scores * step_size[:, None, :]).astype(jnp.bfloat16)
    within = jnp.einsum("hij,jhp->ihp", mixing, values, preferred_element_type=jnp.float32)
    inflow = jnp.exp(cumulative) * (segment_block == prior_segment)[None, :].astype(jnp.float32)
    final_segment = segment_block[-1]
    closing = (
        jnp.exp(cumulative[:, -1:] - cumulative)
        * (segment_block == final_segment)[None, :].astype(jnp.float32)
        * step_size
    )
    weighted = (values.astype(jnp.float32) * closing.T[:, :, None]).astype(jnp.bfloat16)
    writes = jnp.repeat(write_rows, repeat, axis=1)
    deposit = jnp.einsum("jhp,jhn->hpn", weighted, writes, preferred_element_type=jnp.float32)
    fading = jnp.exp(cumulative[:, -1]) * (final_segment == prior_segment).astype(jnp.float32)
    return (within, inflow, fading, deposit)


def reading(read_rows, held_state, repeat):
    readers = jnp.repeat(read_rows, repeat, axis=1).astype(jnp.float32)
    return jnp.einsum("ihn,hpn->ihp", readers, held_state, precision=highest)


def gated_norm(outputs, gates, norm_scale):
    width = INNER // GROUPS
    gated = outputs * jax.nn.silu(gates.astype(jnp.float32))
    pieces = []
    for start in range(0, outputs.shape[1], width):
        group = gated[:, start : start + width]
        mean_square = jnp.mean(group * group, axis=-1, keepdims=True)
        scaled = group * lax.rsqrt(mean_square + 1e-05) * norm_scale[start : start + width]
        pieces.append(scaled.astype(jnp.bfloat16))
    return jnp.concatenate(pieces, axis=1)


def chain_states(fading, deposit):
    half = fading.shape[0] // 2
    count = lax.axis_size("seq")
    swap = [(place, place ^ 1) for place in range(count)]
    second = lax.axis_index("seq") % 2 == 1

    def own(a):
        return jnp.where(second, a[half:], a[:half])

    def partner(a):
        return jnp.where(second, a[:half], a[half:])

    there = own(lax.ppermute(fading, "seq", swap))[:, None, None]
    here = own(fading)[:, None, None]
    other = lax.ppermute(partner(deposit).astype(jnp.bfloat16), "seq", swap).astype(jnp.float32)
    mine = own(deposit)
    early_fade, late_fade = (jnp.where(second, there, here), jnp.where(second, here, there))
    early, late = (jnp.where(second, other, mine), jnp.where(second, mine, other))
    added = late_fade * early + late
    scale = early_fade * late_fade
    carried = passed_along(added.astype(jnp.bfloat16), "seq", 2)
    for _ in range(-(-REACH // 2) - 1):
        held = scale * carried.astype(jnp.float32) + added
        carried = passed_along(held.astype(jnp.bfloat16), "seq", 2)
    first = carried.astype(jnp.float32)
    between = early_fade * first + early
    sent = jnp.where(second, first, between).astype(jnp.bfloat16)
    kept = jnp.where(second, between, first)
    got = lax.ppermute(sent, "seq", swap).astype(jnp.float32)
    return jnp.concatenate([jnp.where(second, got, kept), jnp.where(second, kept, got)])


def on_device(
    inner_input,
    state_input,
    gate_input,
    step_input,
    decay_exponent,
    skip_gain,
    documents,
    filter_inner,
    filter_state,
    norm_gain,
    output_weight,
):
    weight = lax.all_gather(output_weight, "seq", axis=1, tiled=True)
    margin = KERNEL - 1
    length = documents.shape[0]
    head_count = decay_exponent.shape[0]
    groups = state_input.shape[2] // STATE
    repeat = head_count // groups
    channels = inner_input.shape[1]
    state_channels = 2 * state_input.shape[2]
    halo = jnp.concatenate(
        [
            inner_input[-margin:],
            state_input[-margin:].reshape(margin, state_channels),
            jnp.broadcast_to(documents[-margin:, None].astype(jnp.bfloat16), (margin, 128)),
        ],
        axis=1,
    )
    halo = passed_along(halo, "seq", 1)
    before_inner = halo[:, :channels]
    before_state = halo[:, channels : channels + state_channels].reshape(margin, 2, -1)
    before_segments = halo[:, channels + state_channels]
    segments_wide = jnp.concatenate([before_segments.astype(jnp.int32), documents])
    inner_conv = causal_conv(
        jnp.concatenate([before_inner, inner_input]), filter_inner, segments_wide, documents
    )
    state_conv = causal_conv(
        jnp.concatenate([before_state, state_input]), filter_state, segments_wide, documents
    )
    values = inner_conv.reshape(length, head_count, HEAD_DIM)
    write_rows = state_conv[:, 0].reshape(length, groups, STATE)
    read_rows = state_conv[:, 1].reshape(length, groups, STATE)
    step_size = jax.nn.softplus(step_input)
    decay_rate = -step_size * jnp.exp(decay_exponent)[:, None]
    skipped = skip_gain[None, :, None] * values.astype(jnp.float32)
    prior_segment = segments_wide[margin - 1]
    within, inflow, fading, deposit = span_parts(
        values, write_rows, read_rows, step_size, decay_rate, documents, prior_segment
    )
    carried = chain_states(fading, deposit)
    outputs = within + inflow.T[:, :, None] * reading(read_rows, carried, repeat) + skipped
    scan_out = outputs.reshape(length, head_count * HEAD_DIM)
    normed = gated_norm(scan_out, gate_input, norm_gain)
    partial_value = jnp.dot(normed, weight, preferred_element_type=jnp.float32)
    return lax.psum_scatter(
        partial_value.astype(jnp.bfloat16), "head", scatter_dimension=1, tiled=True
    )


def solution(mesh):
    placed = (
        P("seq", "head"),
        P("seq", None, "head"),
        P("seq", "head"),
        P("head", "seq"),
        P("head"),
        P("head"),
        P("seq"),
        P(None, "head"),
        P(None, None, "head"),
        P("head"),
        P("head", "seq"),
    )
    return jax.shard_map(
        on_device, mesh=mesh, in_specs=placed, out_specs=P("seq", "head"), check_vma=False
    )
```

profile of v0, /device:TPU:1, one launch (start us, length us, event | category | flops | bytes accessed | tf_op | source)
XLA Modules:
  0.0 170.2 jit_solution(2397949163513260238)
XLA Ops:
  6.5 0.7 all-gather.2.cloned.1.call-update
  7.3 0.8 slice.128
  8.1 0.7 slice_bitcast_fusion
  8.8 0.7 convert.3
  9.6 4.9 %collective-permute-start = (bf16[3,2688]{1,0:T(4,128)(2,1)S(1)}, bf16[3,2688]{1,0:T(4,128)(2,1)S(1)}, u32[]{:S(2)}, u32[]{:S(2)}) collective-permute-start(bf16[3,2688]{1,0:T(4,128)(2,1)S(1)} %pad_maximum_fusion.2), channel_id=1, source_target_pairs={{0,4},{4,8},{8,12},{12,16},{16,20},{20,24},{24,28},{28,32},{32,36}... | collective-permute-start | bytes 48392 | tf_op jit(solution)/shard_map/ppermute | solution.py:20
  14.6 0.7 exp.32
  15.2 0.8 copy_bitcast_fusion.1
  16.1 0.6 reduce-window.6
  16.8 0.7 slice_bitcast_fusion.4
  17.7 0.9 fusion.32
  18.6 0.2 slice_reduce_fusion.1
  18.8 1.3 slice.157
  20.1 1.1 copy.19
  21.2 0.5 slice.155
  21.8 0.2 copy.18
  23.4 0.8 pad_add_fusion
  24.1 2.0 %slice_compare_fusion.2 = (pred[256]{0:T(512)(128)(4,1)S(1)}, pred[256]{0:T(512)(128)(4,1)S(1)}, pred[256]{0:T(512)(128)(4,1)S(1)}, f32[256]{0:T(256)S(1)}, f32[256]{0:T(256)S(1)}) fusion(s32[256]{0:T(256)} %param.17, s32[259]{0:T(512)S(1)} %pad_add_fusion, s32[]{:T(128)} %bitcast.14, s32[]{:T(128)} %bitcast.16), kind=kLoop, calls=%fused_computation.81 | loop fusion | flops 1792 | bytes 6920 | tf_op jit(solution)/shard_map/eq | solution.py:28
  26.1 0.7 multiply_convert_fusion.3
  27.1 2.1 %multiply_convert_fusion = bf16[256,2048]{1,0:T(8,128)(2,1)S(1)} fusion(bf16[256,2048]{1,0:T(8,128)(2,1)S(1)} %copy-done, bf16[3,2048]{1,0:T(4,128)(2,1)S(1)} %slice.169, f32[2048]{0:T(1024)S(1)} %bitcast.77, f32[2048]{0:T(1024)S(1)} %bitcast.78, f32[2048]{0:T(1024)S(1)} %bitcast.76, f32[2048]{0:T(1024)S(1)} %bitcast.75, ...), kind=kLoop, calls=%fused_computation.16 | loop fusion | flops 14680064 | bytes 2142976 | tf_op jit(solution)/shard_map/convert_element_type | solution.py:31
  29.2 0.5 copy.15
  29.8 0.7 multiply_bitcast_fusion.1
  30.5 0.5 broadcast_in_dim.115
  30.9 0.5 fusion.11
  31.6 0.5 collective-permute-start.1
  32.1 1.0 collective-permute-done.1
  33.4 3.7 %collective-permute-start.3 = (bf16[16,64,128]{2,1,0:T(8,128)(2,1)S(1)}, bf16[16,64,128]{2,1,0:T(8,128)(2,1)S(1)}, u32[]{:S(2)}, u32[]{:S(2)}) collective-permute-start(bf16[16,64,128]{2,1,0:T(8,128)(2,1)S(1)} %get-tuple-element.9), channel_id=1, source_target_pairs={{0,8},{4,12},{8,16},{12,20},{16,24},{20,28},{24,32},{28,36},{32,40... | collective-permute-start | bytes 786440 | tf_op jit(solution)/shard_map/ppermute | solution.py:20
  37.1 9.5 %collective-permute-done.3 = bf16[16,64,128]{2,1,0:T(8,128)(2,1)S(1)} collective-permute-done((bf16[16,64,128]{2,1,0:T(8,128)(2,1)S(1)}, bf16[16,64,128]{2,1,0:T(8,128)(2,1)S(1)}, u32[]{:S(2)}, u32[]{:S(2)}) %collective-permute-start.3) | collective-permute-done | bytes 262176 | tf_op jit(solution)/shard_map/ppermute | solution.py:20
  46.6 0.2 add_convert_fusion.1
  46.8 4.2 %collective-permute-start.4 = (bf16[16,64,128]{2,1,0:T(8,128)(2,1)S(1)}, bf16[16,64,128]{2,1,0:T(8,128)(2,1)S(1)}, u32[]{:S(2)}, u32[]{:S(2)}) collective-permute-start(bf16[16,64,128]{2,1,0:T(8,128)(2,1)S(1)} %add_convert_fusion.1), channel_id=1, source_target_pairs={{0,8},{4,12},{8,16},{12,20},{16,24},{20,28},{24,32},{28,36},{32,40... | collective-permute-start | bytes 786440 | tf_op jit(solution)/shard_map/ppermute | solution.py:20
  51.2 5.1 %collective-permute-done.4 = bf16[16,64,128]{2,1,0:T(8,128)(2,1)S(1)} collective-permute-done((bf16[16,64,128]{2,1,0:T(8,128)(2,1)S(1)}, bf16[16,64,128]{2,1,0:T(8,128)(2,1)S(1)}, u32[]{:S(2)}, u32[]{:S(2)}) %collective-permute-start.4) | collective-permute-done | bytes 262176 | tf_op jit(solution)/shard_map/ppermute | solution.py:20
  56.3 0.2 add_convert_fusion
  56.5 4.1 %collective-permute-start.5 = (bf16[16,64,128]{2,1,0:T(8,128)(2,1)S(1)}, bf16[16,64,128]{2,1,0:T(8,128)(2,1)S(1)}, u32[]{:S(2)}, u32[]{:S(2)}) collective-permute-start(bf16[16,64,128]{2,1,0:T(8,128)(2,1)S(1)} %add_convert_fusion), channel_id=1, source_target_pairs={{0,8},{4,12},{8,16},{12,20},{16,24},{20,28},{24,32},{28,36},{32,40... | collective-permute-start | bytes 786440 | tf_op jit(solution)/shard_map/ppermute | solution.py:20
  60.8 0.3 fusion.34
  61.1 2.4 %fusion.1 = bf16[32,256,256]{2,1,0:T(8,128)(2,1)S(1)} fusion(f32[32,256]{1,0:T(8,128)S(1)} %copy-done.5, f32[2,256,256]{2,1,0:T(8,128)S(1)} %fusion.34, f32[32,256]{1,0:T(8,128)S(1)} %copy-done.3, pred[256,256]{1,0:T(8,128)(4,1)S(1)} %fusion.25), kind=kLoop, calls=%fused_computation.2 | loop fusion | flops 10485760 | bytes 4849664 | tf_op jit(solution)/shard_map/convert_element_type | solution.py:46
  63.5 0.9 collective-permute-done.5
  64.3 0.2 fusion.22
  64.5 6.5 %collective-permute-start.6 = (bf16[16,64,128]{2,1,0:T(8,128)(2,1)S(1)}, bf16[16,64,128]{2,1,0:T(8,128)(2,1)S(1)}, u32[]{:S(2)}, u32[]{:S(2)}) collective-permute-start(bf16[16,64,128]{2,1,0:T(8,128)(2,1)S(1)} %fusion.22), channel_id=1, source_target_pairs={{0,4},{4,0},{8,12},{12,8},{16,20},{20,16},{24,28},{28,24},{32,36},... | collective-permute-start | bytes 786440 | tf_op jit(solution)/shard_map/ppermute | solution.py:107
  71.0 1.4 fusion.35
  72.4 0.2 convert_select_fusion.3
  72.6 0.5 broadcast_in_dim.116
  73.2 3.6 %fusion.3 = f32[256,32,64]{0,2,1:T(8,128)} fusion(bf16[256,32,64]{0,2,1:T(8,128)(2,1)S(1)} %bitcast.66, f32[32,64,256]{2,1,0:T(8,128)S(1)} %fusion.35, bf16[256,32,128]{2,0,1:T(8,128)(2,1)S(1)} %bitcast.68, f32[16,64,128]{2,1,0:T(8,128)S(1)} %get-tuple-element.14, f32[16,64,128]{2,1,0:T(8,128)S(1)} %get-tuple-element.13, f32[32]{0:T(128)S(1)} %copy-done.9, ...), kind=kOutput, calls=%fused_computation.9 | convolution fusion | flops 808189952 | bytes 8421504 | tf_op jit(solution)/shard_map/ihn,hpn->ihp/dot_general | solution.py:64
  76.8 2.2 %copy.25 = f32[256,2048]{1,0:T(8,128)S(1)} copy(f32[256,2048]{0,1:T(8,128)} %bitcast.69) | data formatting | bytes 4194304 | tf_op jit(solution)/shard_map/reshape | solution.py:163
  79.0 0.6 fusion.7
  79.6 0.2 multiply_reduce_fusion.1
  79.8 0.3 multiply_convert_fusion.2
  80.1 35.4 %all-gather.2.cloned.1.call-done = bf16[2048,4096]{0,1:T(8,128)(2,1)} async-done(((bf16[2048,64]{0,1:T(8,128)(2,1)}), bf16[2048,4096]{0,1:T(8,128)(2,1)}) %all-gather.2.cloned.1.call-update) | async-done | bytes 16777232 | tf_op jit(solution)/shard_map/all_gather | solution.py:124
  115.4 18.1 %convolution_convert_fusion = bf16[256,4096]{1,0:T(8,128)(2,1)} fusion(bf16[2048,4096]{0,1:T(8,128)(2,1)} %all-gather.2.cloned.1.call-done, bf16[256,1024]{1,0:T(8,128)(2,1)S(1)} %get-tuple-element.12, bf16[256,1024]{1,0:T(8,128)(2,1)S(1)} %get-tuple-element.11), kind=kOutput, calls=%fused_computation.3 | convolution fusion | flops 4298113024 | bytes 19922944 | tf_op jit(solution)/shard_map/dot_general | solution.py:165
  133.5 29.8 %reduce-scatter.2.cloned.1.call-done = bf16[256,1024]{1,0:T(8,128)(2,1)} async-done(((bf16[256,4096]{1,0:T(8,128)(2,1)}), bf16[256,1024]{1,0:T(8,128)(2,1)}) %reduce-scatter.2.cloned.1.call-update) | async-done | bytes 524304 | tf_op jit(solution)/shard_map/reduce_scatter | solution.py:166
  (49 shorter events, 1.5 us)
Async XLA Ops:
  6.5 20.5 %copy-start = (bf16[256,2048]{1,0:T(8,128)(2,1)S(1)}, bf16[256,2048]{1,0:T(8,128)(2,1)}, u32[]{:S(2)}) copy-start(bf16[256,2048]{1,0:T(8,128)(2,1)} %param.11) | copy-start | bytes 3145732
  6.5 108.9 %all-gather.2.cloned.1.call-start = ((), (), s32[]{:S(2)}) async-start(), calls=%async_computation.1 | async-start | bytes 17039360 | tf_op jit(solution)/shard_map/all_gather | solution.py:124
  7.3 156.1 %reduce-scatter.2.cloned.1.call-start = ((), (), s32[]{:S(2)}) async-start(), calls=%async_computation.2 | async-start | bytes 2621440 | tf_op jit(solution)/shard_map/reduce_scatter | solution.py:166
  9.6 11.6 %collective-permute-start = (bf16[3,2688]{1,0:T(4,128)(2,1)S(1)}, bf16[3,2688]{1,0:T(4,128)(2,1)S(1)}, u32[]{:S(2)}, u32[]{:S(2)}) collective-permute-start(bf16[3,2688]{1,0:T(4,128)(2,1)S(1)} %pad_maximum_fusion.2), channel_id=1, source_target_pairs={{0,4},{4,8},{8,12},{12,16},{16,20},{20,24},{24,28},{28,32},{32,36}... | collective-permute-start | bytes 48392 | tf_op jit(solution)/shard_map/ppermute | solution.py:20
  17.7 1.1 copy-start.2
  27.1 2.7 %copy-start.6 = (f32[32,256]{1,0:T(8,128)S(1)}, f32[32,256]{1,0:T(8,128)}, u32[]{:S(2)}) copy-start(f32[32,256]{1,0:T(8,128)} %param.14) | copy-start | bytes 98308
  31.4 19.6 %copy-start.7 = (s32[256]{0:T(256)S(1)}, s32[256]{0:T(256)}, u32[]{:S(2)}) copy-start(s32[256]{0:T(256)} %param.17) | copy-start | bytes 3076
  31.5 1.7 collective-permute-start.2
  31.6 1.5 collective-permute-start.1
  33.2 27.4 %copy-start.8 = (f32[2048]{0:T(1024)S(1)}, f32[2048]{0:T(1024)}, u32[]{:S(2)}) copy-start(f32[2048]{0:T(1024)} %param.20) | copy-start | bytes 24580
  33.4 27.7 %copy-start.3 = (f32[32,256]{1,0:T(8,128)S(1)}, f32[32,256]{1,0:T(8,128)}, u32[]{:S(2)}) copy-start(f32[32,256]{1,0:T(8,128)} %copy-done.2) | copy-start | bytes 98308
  33.4 27.7 %copy-start.5 = (f32[32,256]{1,0:T(8,128)S(1)}, f32[32,256]{1,0:T(8,128)}, u32[]{:S(2)}) copy-start(f32[32,256]{1,0:T(8,128)} %get-tuple-element.19) | copy-start | bytes 98308
  33.4 13.2 %collective-permute-start.3 = (bf16[16,64,128]{2,1,0:T(8,128)(2,1)S(1)}, bf16[16,64,128]{2,1,0:T(8,128)(2,1)S(1)}, u32[]{:S(2)}, u32[]{:S(2)}) collective-permute-start(bf16[16,64,128]{2,1,0:T(8,128)(2,1)S(1)} %get-tuple-element.9), channel_id=1, source_target_pairs={{0,8},{4,12},{8,16},{12,20},{16,24},{20,28},{24,32},{28,36},{32,40... | collective-permute-start | bytes 786440 | tf_op jit(solution)/shard_map/ppermute | solution.py:20
  46.8 9.5 %collective-permute-start.4 = (bf16[16,64,128]{2,1,0:T(8,128)(2,1)S(1)}, bf16[16,64,128]{2,1,0:T(8,128)(2,1)S(1)}, u32[]{:S(2)}, u32[]{:S(2)}) collective-permute-start(bf16[16,64,128]{2,1,0:T(8,128)(2,1)S(1)} %add_convert_fusion.1), channel_id=1, source_target_pairs={{0,8},{4,12},{8,16},{12,20},{16,24},{20,28},{24,32},{28,36},{32,40... | collective-permute-start | bytes 786440 | tf_op jit(solution)/shard_map/ppermute | solution.py:20
  56.5 7.8 %collective-permute-start.5 = (bf16[16,64,128]{2,1,0:T(8,128)(2,1)S(1)}, bf16[16,64,128]{2,1,0:T(8,128)(2,1)S(1)}, u32[]{:S(2)}, u32[]{:S(2)}) collective-permute-start(bf16[16,64,128]{2,1,0:T(8,128)(2,1)S(1)} %add_convert_fusion), channel_id=1, source_target_pairs={{0,8},{4,12},{8,16},{12,20},{16,24},{20,28},{24,32},{28,36},{32,40... | collective-permute-start | bytes 786440 | tf_op jit(solution)/shard_map/ppermute | solution.py:20
  64.5 7.9 %collective-permute-start.6 = (bf16[16,64,128]{2,1,0:T(8,128)(2,1)S(1)}, bf16[16,64,128]{2,1,0:T(8,128)(2,1)S(1)}, u32[]{:S(2)}, u32[]{:S(2)}) collective-permute-start(bf16[16,64,128]{2,1,0:T(8,128)(2,1)S(1)} %fusion.22), channel_id=1, source_target_pairs={{0,4},{4,0},{8,12},{12,8},{16,20},{20,16},{24,28},{28,24},{32,36},... | collective-permute-start | bytes 786440 | tf_op jit(solution)/shard_map/ppermute | solution.py:107
  72.4 0.8 copy-start.4
  72.4 0.8 copy-start.9
  76.8 2.2 %copy-start.1 = (bf16[256,2048]{1,0:T(8,128)(2,1)S(1)}, bf16[256,2048]{1,0:T(8,128)(2,1)}, u32[]{:S(2)}) copy-start(bf16[256,2048]{1,0:T(8,128)(2,1)} %param.13) | copy-start | bytes 3145732
Sparse Core Ops, SparseCore 0:
  10.1 105.2 all-gather.1
  133.6 29.6 reduce-scatter.1
where the time goes:
time: 171 us; the launch traced here: 170 us
  waiting for transfers between devices  82.4 us (48%)
  starting transfers between devices  24.1 us (14%)
  matrix products  23.8 us (14%)
  between operations  15.1 us (9%)
  other arithmetic  13.4 us (8%)
  local copies, waits for them, and re-layouts  11.4 us (7%)
    all_gather x1, waiting for transfers between devices, on_device(): weight = lax.all_gather(output_weight, 'seq', axis=1, tiled=True)  35.4 us
    reduce_scatter x1, waiting for transfers between devices, on_device(): lax.psum_scatter(partial_value.astype(jnp.bfloat16), 'head', scatter_dime...  29.8 us
    dot_general x1, matrix products, on_device(): partial_value = jnp.dot(normed, weight, preferred_element_type=jnp.float32)  18.1 us
    ppermute x4, starting transfers between devices, passed_along(): lax.ppermute(value, axis, [(source, source + steps) for source in range(i...  17 us
    ppermute x4, waiting for transfers between devices, passed_along(): lax.ppermute(value, axis, [(source, source + steps) for source in range(i...  15.5 us
    ppermute x1, starting transfers between devices, chain_states(): got = lax.ppermute(sent, 'seq', swap).astype(jnp.float32)  6.52 us
    dot_general x1, matrix products, reading(): return jnp.einsum('ihn,hpn->ihp', readers, held_state, precision=highest)  3.64 us
  transfers between devices with their start and end apart: 9, of which 6 were waited for; matrix products, arithmetic and copies ran while one was open for 18% of the time, Pallas kernels for 0%

commit v1 on v0

--- a/solution.py
+++ b/solution.py
@@ -1,3 +1,4 @@
+import functools
 import jax
 import jax.numpy as jnp
 from jax import lax
@@ -12,6 +13,16 @@
 DOC_MOST = 1536
 REACH = -(-(DOC_MOST - 1) // SPAN)
 highest = lax.Precision.HIGHEST
+
+
+def switch_samples(field_in, dim_at):
+    return jnp.concatenate(
+        jax.lax.all_to_all(jnp.stack([field_in] * jax.lax.axis_size("seq")), "seq", 0, 0),
+        axis=dim_at,
+    )
+
+
+change_the_unit = functools.partial(switch_samples, dim_at=1)
 
 
 def passed_along(value, axis, steps):
@@ -121,7 +132,7 @@
     norm_gain,
     output_weight,
 ):
-    weight = lax.all_gather(output_weight, "seq", axis=1, tiled=True)
+    weight = change_the_unit(output_weight)
     margin = KERNEL - 1
     length = documents.shape[0]
     head_count = decay_exponent.shape[0]

time: 171 us -> 499 us (2.92)
  waiting for transfers between devices: 82.4 us -> 403 us
  starting transfers between devices: 24.1 us -> 33.7 us
    ppermute x4, waiting for transfers between devices: 15.5 us -> 363 us  [passed_along(): lax.ppermute(value, axis, [(source, source + steps) for source in range(i...]
    all_gather x1 -> x0, waiting for transfers between devices: 35.4 us -> none  [on_device(): weight = lax.all_gather(output_weight, 'seq', axis=1, tiled=True)]
    all_to_all x0 -> x1, starting transfers between devices: none -> 13.5 us  [switch_samples(): jax.lax.all_to_all(jnp.stack([field_in] * jax.lax.axis_size('seq')), 'seq...]
    reduce_scatter x1, waiting for transfers between devices: 29.8 us -> 38.7 us  [on_device(): lax.psum_scatter(partial_value.astype(jnp.bfloat16), 'head', scatter_dime...]
    another operation x1 -> x2, local copies, waits for them, and re-layouts: 0.01 us -> 6.72 us  [the longest x1 6.72 us: switch_samples(): jnp.stack([field_in] * jax.lax.axis_size('seq'))]
  transfers between devices with their start and end apart: 9 -> 9, of which waited for: 6 -> 6; matrix products, arithmetic and copies ran while one was open for 18% -> 4% of each run, Pallas kernels for 0% -> 0%
where the time goes in v1:
time: 499 us
  waiting for transfers between devices  403 us (81%)
  starting transfers between devices  33.7 us (7%)
  matrix products  23.8 us (5%)
  between operations  15.2 us (3%)
  local copies, waits for them, and re-layouts  12.6 us (3%)
  other arithmetic  10.5 us (2%)
    ppermute x4, waiting for transfers between devices, passed_along(): lax.ppermute(value, axis, [(source, source + steps) for source in range(i...  363 us
    reduce_scatter x1, waiting for transfers between devices, on_device(): lax.psum_scatter(partial_value.astype(jnp.bfloat16), 'head', scatter_dime...  38.7 us
    dot_general x1, matrix products, on_device(): partial_value = jnp.dot(normed, weight, preferred_element_type=jnp.float32)  18.1 us
    ppermute x4, starting transfers between devices, passed_along(): lax.ppermute(value, axis, [(source, source + steps) for source in range(i...  16.4 us
    all_to_all x1, starting transfers between devices, switch_samples(): jax.lax.all_to_all(jnp.stack([field_in] * jax.lax.axis_size('seq')), 'seq...  13.5 us
  transfers between devices with their start and end apart: 9, of which 6 were waited for; matrix products, arithmetic and copies ran while one was open for 4% of the time, Pallas kernels for 0%

profile of v1, /device:TPU:1, one launch (start us, length us, event | category | flops | bytes accessed | tf_op | source)
XLA Modules:
  0.0 498.6 jit_solution(13407632714855091330)
XLA Ops:
  6.5 6.7 %stack.2 = bf16[64,2048,64]{1,2,0:T(8,128)(2,1)} broadcast(bf16[2048,64]{0,1:T(8,128)(2,1)} %param.21), dimensions={1,2} | broadcast | bytes 17039360 | tf_op jit(solution)/shard_map/stack | solution.py:20
  13.3 13.5 %all-to-all-start = ((bf16[64,2048,64]{1,2,0:T(8,128)(2,1)}), bf16[64,2048,64]{1,2,0:T(8,128)(2,1)}, u32[]{:S(2)}, u32[]{:S(2)}) async-start(bf16[64,2048,64]{1,2,0:T(8,128)(2,1)} %stack.2), calls=%async_computation | async-start | bytes 33554432 | tf_op jit(solution)/shard_map/all_to_all | solution.py:20
  27.1 3.5 collective-permute-start
  30.7 0.6 reduce-window.6
  31.3 0.2 slice_reduce_fusion
  31.7 0.2 slice_reduce_fusion.1
  31.8 0.7 slice.157
  32.5 0.2 copy.20
  32.7 352.7 %collective-permute-done = bf16[3,2688]{1,0:T(4,128)(2,1)S(1)} collective-permute-done((bf16[3,2688]{1,0:T(4,128)(2,1)S(1)}, bf16[3,2688]{1,0:T(4,128)(2,1)S(1)}, u32[]{:S(2)}, u32[]{:S(2)}) %collective-permute-start) | collective-permute-done | bytes 16160 | tf_op jit(solution)/shard_map/ppermute | solution.py:31
  385.4 0.5 slice.155
  387.3 0.1 fusion.27
  387.5 1.4 slice_compare_fusion.2
  388.9 2.1 multiply_convert_fusion
  391.0 0.5 copy.16
  391.5 0.2 copy.19
  391.7 0.7 multiply_convert_fusion.3
  392.5 0.1 copy.24
  392.6 0.7 multiply_bitcast_fusion.1
  393.3 0.5 broadcast_in_dim.115
  393.8 0.5 fusion.11
  394.3 0.1 collective-permute-start.2
  394.5 0.5 collective-permute-start.1
  394.9 1.0 collective-permute-done.1
  396.0 0.2 fusion.30
  396.2 4.6 collective-permute-start.3
  400.8 5.3 %collective-permute-done.3 = bf16[16,64,128]{2,1,0:T(8,128)(2,1)S(1)} collective-permute-done((bf16[16,64,128]{2,1,0:T(8,128)(2,1)S(1)}, bf16[16,64,128]{2,1,0:T(8,128)(2,1)S(1)}, u32[]{:S(2)}, u32[]{:S(2)}) %collective-permute-start.3) | collective-permute-done | bytes 262176 | tf_op jit(solution)/shard_map/ppermute | solution.py:31
  406.1 0.2 add_convert_fusion.1
  406.3 4.1 collective-permute-start.4
  410.4 0.1 fusion.25
  410.6 4.3 collective-permute-done.4
  414.9 0.2 add_convert_fusion
  415.1 4.1 collective-permute-start.5
  419.2 0.1 copy.25
  419.4 0.3 fusion.34
  419.7 2.3 fusion.1
  422.0 0.8 collective-permute-done.5
  422.8 0.2 fusion.22
  422.9 3.2 collective-permute-start.6
  426.1 1.4 fusion.35
  427.6 0.2 convert_select_fusion.3
  427.8 0.5 broadcast_in_dim.116
  428.3 3.6 fusion.3
  431.9 2.0 copy.26
  433.9 0.6 fusion.7
  434.5 0.2 multiply_reduce_fusion.1
  434.7 0.3 multiply_convert_fusion.2
  435.0 18.1 %convolution_convert_fusion = bf16[256,4096]{1,0:T(8,128)(2,1)} fusion(bf16[2048,4096]{0,1:T(8,128)(2,1)} %bitcast.23, bf16[256,1024]{1,0:T(8,128)(2,1)S(1)} %get-tuple-element.12, bf16[256,1024]{1,0:T(8,128)(2,1)S(1)} %get-tuple-element.11), kind=kOutput, calls=%fused_computation.3 | convolution fusion | flops 4298113024 | bytes 19922944 | tf_op jit(solution)/shard_map/dot_general | solution.py:176
  453.1 38.7 %reduce-scatter.2.cloned.1.call-done = bf16[256,1024]{1,0:T(8,128)(2,1)} async-done(((bf16[256,4096]{1,0:T(8,128)(2,1)}), bf16[256,1024]{1,0:T(8,128)(2,1)}) %reduce-scatter.2.cloned.1.call-update) | async-done | bytes 524304 | tf_op jit(solution)/shard_map/reduce_scatter | solution.py:177
  (57 shorter events, 0.8 us)
Async XLA Ops:
  13.3 13.6 %copy-start.9 = (s32[256]{0:T(256)S(1)}, s32[256]{0:T(256)}, u32[]{:S(2)}) copy-start(s32[256]{0:T(256)} %param.17) | copy-start | bytes 3076
  13.3 13.7 %copy-start.4 = (bf16[256,2,256]{2,1,0:T(2,128)(2,1)S(1)}, bf16[256,2,256]{2,1,0:T(2,128)(2,1)}, u32[]{:S(2)}) copy-start(bf16[256,2,256]{2,1,0:T(2,128)(2,1)} %param.12) | copy-start | bytes 786436
  13.3 13.7 %copy-start = (bf16[256,2048]{1,0:T(8,128)(2,1)S(1)}, bf16[256,2048]{1,0:T(8,128)(2,1)}, u32[]{:S(2)}) copy-start(bf16[256,2048]{1,0:T(8,128)(2,1)} %param.11) | copy-start | bytes 3145732
  13.3 17.4 %copy-start.13 = (f32[32]{0:T(128)S(1)}, f32[32]{0:T(128)}, u32[]{:S(2)}) copy-start(f32[32]{0:T(128)} %param.15) | copy-start | bytes 388
  13.3 17.4 %copy-start.7 = (f32[32,256]{1,0:T(8,128)S(1)}, f32[32,256]{1,0:T(8,128)}, u32[]{:S(2)}) copy-start(f32[32,256]{1,0:T(8,128)} %param.14) | copy-start | bytes 98308
  13.3 18.2 %copy-start.10 = (f32[4,2,256]{2,1,0:T(2,128)S(1)}, f32[4,2,256]{2,1,0:T(2,128)}, u32[]{:S(2)}) copy-start(f32[4,2,256]{2,1,0:T(2,128)} %param.19) | copy-start | bytes 24580
  13.3 18.3 %copy-start.8 = (f32[4,2048]{1,0:T(4,128)S(1)}, f32[4,2048]{1,0:T(4,128)}, u32[]{:S(2)}) copy-start(f32[4,2048]{1,0:T(4,128)} %param.18) | copy-start | bytes 98308
  13.3 421.7 %all-to-all-start = ((bf16[64,2048,64]{1,2,0:T(8,128)(2,1)}), bf16[64,2048,64]{1,2,0:T(8,128)(2,1)}, u32[]{:S(2)}, u32[]{:S(2)}) async-start(bf16[64,2048,64]{1,2,0:T(8,128)(2,1)} %stack.2), calls=%async_computation | async-start | bytes 33554432 | tf_op jit(solution)/shard_map/all_to_all | solution.py:20
  26.8 465.0 %reduce-scatter.2.cloned.1.call-start = ((), (), s32[]{:S(2)}) async-start(), calls=%async_computation.2 | async-start | bytes 2621440 | tf_op jit(solution)/shard_map/reduce_scatter | solution.py:177
  27.1 358.3 %collective-permute-start = (bf16[3,2688]{1,0:T(4,128)(2,1)S(1)}, bf16[3,2688]{1,0:T(4,128)(2,1)S(1)}, u32[]{:S(2)}, u32[]{:S(2)}) collective-permute-start(bf16[3,2688]{1,0:T(4,128)(2,1)S(1)} %pad_maximum_fusion.2), channel_id=1, source_target_pairs={{0,4},{4,8},{8,12},{12,16},{16,20},{20,24},{24,28},{28,32},{32,36}... | collective-permute-start | bytes 48392 | tf_op jit(solution)/shard_map/ppermute | solution.py:31
  31.6 357.3 %copy-start.2 = (f32[32,256]{1,0:T(8,128)}, f32[32,256]{1,0:T(8,128)S(1)}, u32[]{:S(2)}) copy-start(f32[32,256]{1,0:T(8,128)S(1)} %copy_bitcast_fusion) | copy-start | bytes 98308
  394.3 1.7 collective-permute-start.2
  394.5 1.5 collective-permute-start.1
  396.0 23.2 %copy-start.11 = (f32[2048]{0:T(1024)S(1)}, f32[2048]{0:T(1024)}, u32[]{:S(2)}) copy-start(f32[2048]{0:T(1024)} %param.20) | copy-start | bytes 24580
  396.2 23.4 %copy-start.3 = (f32[32,256]{1,0:T(8,128)S(1)}, f32[32,256]{1,0:T(8,128)}, u32[]{:S(2)}) copy-start(f32[32,256]{1,0:T(8,128)} %copy-done.2) | copy-start | bytes 98308
  396.2 23.4 %copy-start.6 = (f32[32,256]{1,0:T(8,128)S(1)}, f32[32,256]{1,0:T(8,128)}, u32[]{:S(2)}) copy-start(f32[32,256]{1,0:T(8,128)} %get-tuple-element.19) | copy-start | bytes 98308
  396.2 9.9 %collective-permute-start.3 = (bf16[16,64,128]{2,1,0:T(8,128)(2,1)S(1)}, bf16[16,64,128]{2,1,0:T(8,128)(2,1)S(1)}, u32[]{:S(2)}, u32[]{:S(2)}) collective-permute-start(bf16[16,64,128]{2,1,0:T(8,128)(2,1)S(1)} %get-tuple-element.9), channel_id=1, source_target_pairs={{0,8},{4,12},{8,16},{12,20},{16,24},{20,28},{24,32},{28,36},{32,40... | collective-permute-start | bytes 786440 | tf_op jit(solution)/shard_map/ppermute | solution.py:31
  406.3 8.5 %collective-permute-start.4 = (bf16[16,64,128]{2,1,0:T(8,128)(2,1)S(1)}, bf16[16,64,128]{2,1,0:T(8,128)(2,1)S(1)}, u32[]{:S(2)}, u32[]{:S(2)}) collective-permute-start(bf16[16,64,128]{2,1,0:T(8,128)(2,1)S(1)} %add_convert_fusion.1), channel_id=1, source_target_pairs={{0,8},{4,12},{8,16},{12,20},{16,24},{20,28},{24,32},{28,36},{32,40... | collective-permute-start | bytes 786440 | tf_op jit(solution)/shard_map/ppermute | solution.py:31
  415.1 7.7 %collective-permute-start.5 = (bf16[16,64,128]{2,1,0:T(8,128)(2,1)S(1)}, bf16[16,64,128]{2,1,0:T(8,128)(2,1)S(1)}, u32[]{:S(2)}, u32[]{:S(2)}) collective-permute-start(bf16[16,64,128]{2,1,0:T(8,128)(2,1)S(1)} %add_convert_fusion), channel_id=1, source_target_pairs={{0,8},{4,12},{8,16},{12,20},{16,24},{20,28},{24,32},{28,36},{32,40... | collective-permute-start | bytes 786440 | tf_op jit(solution)/shard_map/ppermute | solution.py:31
  422.9 4.6 collective-permute-start.6
  427.5 0.8 copy-start.5
  427.5 0.8 copy-start.12
  431.9 2.0 copy-start.1
Sparse Core Ops, SparseCore 0:
  453.2 38.5 reduce-scatter.1
